TPU v7x, 32 devices: a whole 2x2x4 slice. The times are simulated.
32 devices in a mesh: dev: 32 (over z, y, x, core).
Axes of the slice: x: 2, y: 2, z: 4, core: 2. Of those that a mesh axis runs over, the one named last changes fastest.
Arguments:
- features: bfloat16 [16384, 1024], P('dev'), may hold values from -6 to 6
- w_hidden: bfloat16 [1024, 512], replicated, may hold values from -0.1875 to 0.1875
- w_out: bfloat16 [512, 128], replicated, may hold values from -0.25 to 0.25
- items: bfloat16 [65536, 128], P('dev'), may hold values from -200 to 200
- routes: int32 [16384, 4], P('dev'), may hold values from 0 to 511, all different within a row; in each aligned block of 512 rows (0 to 511, 512 to 1023, ...) at most 8 rows name the same one
- cluster_slot: int32 [512], replicated, may hold values from 0 to 511, each once
- sample_ids: int32 [512, 4096], P('dev'), may hold values from 0 to 127
- sample_counts: int32 [512, 4096], P('dev'), may hold values from 1 to 4095
- positives: int32 [16384, 4], P('dev'), may hold values from 0 to 4095
Outputs:
- slot_loss: float32 [512], P('dev')
- grad_hidden: float32 [1024, 512], replicated
- grad_out: float32 [512, 128], replicated
- item_grad: float32 [65536, 128], P('dev')
Inputs may be any that keep to these rules, and one draw needn't show every extreme that they name: `routes`: each row names 4 different clusters; within the rows of one device no cluster is named more than 8 times; every cluster is named by some row. `cluster_slot`: each cluster has one slot.
All inputs are finite; a program needn't handle non-finite values.
Results may differ from a plain program's by a relative error of at most 0.012.
The roundings to bfloat16 on the way count: a program that leaves them out, or rounds other values in their place, can miss the bound.
Values may be sent and summed in bfloat16 or wider, within the bound.
A program may use at most 128 MiB of HBM per device.

v0:
```python
import functools

import jax
import jax.numpy as jnp
from jax import lax
from jax.experimental import pallas as pl
from jax.experimental.pallas import tpu as pltpu
from jax.sharding import PartitionSpec as P


def silu_grad(value):
    sig = jax.nn.sigmoid(value)
    return sig * (1.0 + value * (1.0 - sig))


def slot_codes(routes_t, positives, cluster_slot, capacity):
    visits, users = routes_t.shape
    clusters = cluster_slot.shape[0]
    ids = lax.broadcasted_iota(jnp.int32, (visits, clusters, users), 1)
    slots = jnp.sum(
        jnp.where(routes_t[:, None, :] == ids, cluster_slot[None, :, None], 0), axis=1
    )
    rows = lax.broadcasted_iota(jnp.int32, (clusters, users), 0)
    columns = lax.broadcasted_iota(jnp.int32, (users, clusters), 1)
    slots_u = slots.T
    member = jnp.zeros((clusters, users), jnp.bool_)
    member_u = jnp.zeros((users, clusters), jnp.bool_)
    target_u = jnp.zeros((users, clusters), jnp.int32)
    for r in range(visits):
        member = member | (slots[r][None, :] == rows)
        same = slots_u[:, r][:, None] == columns
        member_u = member_u | same
        target_u = jnp.where(same, positives[:, r][:, None] + 1, target_u)
    first = lax.broadcasted_iota(jnp.int32, (users, users), 0)
    second = lax.broadcasted_iota(jnp.int32, (users, users), 1)
    rank = jnp.dot(
        member.astype(jnp.bfloat16),
        (first < second).astype(jnp.bfloat16),
        preferred_element_type=jnp.float32,
    )
    rank_u = jnp.dot(
        (second < first).astype(jnp.bfloat16),
        member_u.astype(jnp.bfloat16),
        preferred_element_type=jnp.float32,
    )
    code = jnp.where(member, rank, -1.0).astype(jnp.bfloat16)
    code_u = jnp.where(member_u, rank_u, -1.0)
    seats = lax.broadcasted_iota(jnp.int32, (capacity, 1, 1), 0).astype(jnp.float32)
    return code, jnp.sum(jnp.where(code_u[None] == seats, target_u[None], 0), axis=1)


def owner(queries, targets, block_items, table_ids, counts):
    clusters, samples = table_ids.shape
    item_rows = block_items.shape[1]
    recip = 1.0 / counts.astype(jnp.float32)
    which = lax.broadcasted_iota(jnp.int32, (clusters, item_rows, samples), 1)
    mass = jnp.sum(jnp.where(table_ids[:, None, :] == which, recip[:, None, :], 0.0), axis=2)
    log_mass = jnp.log(mass)
    lanes = 128
    groups = samples // lanes
    low = targets % lanes
    high = targets // lanes
    pick_low = (
        low[:, :, None] == lax.broadcasted_iota(jnp.int32, low.shape + (lanes,), 2)
    ).astype(jnp.bfloat16)
    table = jnp.concatenate([table_ids, counts // 64, counts % 64], axis=1)
    table = table.reshape(clusters, 3 * groups, lanes).astype(jnp.bfloat16)
    near = jnp.einsum("cql,chl->cqh", pick_low, table, preferred_element_type=jnp.float32)
    column = lax.broadcasted_iota(jnp.int32, near.shape, 2)
    parts = [
        jnp.sum(jnp.where(column == high[:, :, None] + groups * t, near, 0.0), axis=2)
        for t in range(3)
    ]
    live = targets >= 0
    own_id = parts[0].astype(jnp.int32)
    own_count = jnp.where(live, parts[1] * 64.0 + parts[2], 1.0)
    scores = jnp.einsum("cqe,cie->cqi", queries, block_items, preferred_element_type=jnp.float32)
    shifted = scores + log_mass[:, None, :]
    top = jnp.max(shifted, axis=2, keepdims=True)
    expo = jnp.exp(shifted - top)
    total = jnp.sum(expo, axis=2, keepdims=True)
    hit = (
        lax.broadcasted_iota(jnp.int32, scores.shape, 2)
        == jnp.where(live, own_id, -1)[:, :, None]
    )
    picked = jnp.sum(jnp.where(hit, scores, 0.0), axis=2) - jnp.log(own_count)
    losses = jnp.log(total[:, :, 0]) + top[:, :, 0] - picked
    cluster_loss = jnp.sum(jnp.where(live, losses, 0.0), axis=1) / jnp.sum(
        live.astype(jnp.float32), axis=1
    )
    wsum = expo / total - hit.astype(jnp.float32)
    coarse = lax.reduce_precision(wsum, 8, 7)
    fine = (wsum - coarse).astype(jnp.bfloat16)
    coarse = coarse.astype(jnp.bfloat16)

    def both(equation, other):
        return jnp.einsum(
            equation, coarse, other, preferred_element_type=jnp.float32
        ) + jnp.einsum(equation, fine, other, preferred_element_type=jnp.float32)

    dquery = both("cqi,cie->cqe", block_items).astype(jnp.bfloat16)
    dtable = both("cqi,cqe->cie", queries)
    return cluster_loss, dquery, dtable


ORDERS = 3
TILE = 16


def row_groups(bits, tiles):
    turn = [b for b in (1, 2, 3) if b < bits]
    rest = [b for b in range(bits) if b > 3]
    shares = [tiles] if tiles == 1 else [tiles - tiles // 2, tiles // 2]
    groups = []
    start = 0
    for share in shares:
        for k in range(ORDERS):
            k = k % max(1, len(turn))
            size = (share * TILE) << bits
            groups.append((start, size, [0] + turn[k:] + turn[:k] + rest))
            start += size
    return groups


def pieces_of(refs, start, size):
    row = 0
    for ref in refs:
        rows, columns = ref.shape
        for c in range(columns // 128):
            low, high = max(start, row), min(start + size, row + rows)
            if low < high:
                yield low, high, ref.at[low - row : high - row, c * 128 : (c + 1) * 128]
            row += rows
    low = max(start, row)
    if low < start + size:
        yield low, start + size, None


def reduce_kernel(bits, tiles, big_ref, small_ref, big_out, small_out, acc, out, inbox, full, send, recv):
    me = lax.axis_index("dev")
    mesh = pl.DeviceIdType.MESH
    groups = row_groups(bits, tiles)
    bit = [(me // (1 << b)) % 2 for b in range(bits)]
    partners = [me + (1 << b) * (1 - 2 * bit[b]) for b in range(bits)]

    barrier = pltpu.get_barrier_semaphore()
    for b in range(bits):
        pl.semaphore_signal(barrier, inc=1, device_id=(partners[b],), device_id_type=mesh)
    def rows_at(first, count):
        return pl.ds(pl.multiple_of(first, TILE), count)

    off = [start for start, _, _ in groups]
    length = [size for _, size, _ in groups]
    waiting = [None] * len(groups)
    landed = [0] * len(groups)
    started = []

    def take(g):
        waiting[g].wait_recv()
        kept = rows_at(off[g], length[g])
        got = inbox[pl.ds(groups[g][0] + landed[g], length[g]), :].astype(jnp.float32)
        acc[kept, :] = acc[kept, :] + got
        landed[g] += length[g]

    for s in range(bits):
        for g in range(len(groups)):
            start, size, order = groups[g]
            if s > 0:
                take(g)
            else:
                for low, high, part in pieces_of((big_ref, small_ref), start, size):
                    blank = jnp.zeros((high - low, 128), jnp.float32)
                    acc[low:high, :] = blank if part is None else part[...]
            b = order[s]
            half = length[g] // 2
            give = off[g] + (1 - bit[b]) * half
            off[g] = off[g] + bit[b] * half
            length[g] = half
            out[rows_at(give, half), :] = acc[rows_at(give, half), :].astype(jnp.bfloat16)
            if s == 0 and g == 0:
                pl.semaphore_wait(barrier, bits)
            copy = pltpu.make_async_remote_copy(
                src_ref=out.at[rows_at(give, half), :],
                dst_ref=inbox.at[pl.ds(start + landed[g], half), :],
                send_sem=send.at[g, s],
                recv_sem=recv.at[g, s],
                device_id=(partners[b],),
                device_id_type=mesh,
            )
            copy.start()
            waiting[g] = copy
            started.append(copy)
    for s in range(bits - 1, -1, -1):
        for g in range(len(groups)):
            if s == bits - 1:
                take(g)
                kept = rows_at(off[g], length[g])
                full[kept, :] = acc[kept, :].astype(jnp.bfloat16)
            else:
                waiting[g].wait_recv()
            b = groups[g][2][s]
            held = rows_at(off[g], length[g])
            copy = pltpu.make_async_remote_copy(
                src_ref=full.at[held, :],
                dst_ref=full.at[held, :],
                send_sem=send.at[g, bits + s],
                recv_sem=recv.at[g, bits + s],
                device_id=(partners[b],),
                device_id_type=mesh,
            )
            copy.start()
            waiting[g] = copy
            started.append(copy)
            off[g] = off[g] - bit[b] * length[g]
            length[g] = length[g] * 2
    for g in range(len(groups)):
        waiting[g].wait_recv()
        for low, high, part in pieces_of((big_out, small_out), groups[g][0], groups[g][1]):
            if part is not None:
                part[...] = full[low:high, :]
    for copy in started:
        copy.wait_send()


def sum_over_devices(big, small):
    devices = lax.axis_size("dev")
    bits = devices.bit_length() - 1
    tiles = -(-((big.size + small.size) // 128) // (ORDERS * devices * TILE))
    groups = row_groups(bits, tiles)
    rows = groups[-1][0] + groups[-1][1]
    summed = pl.pallas_call(
        functools.partial(reduce_kernel, bits, tiles),
        out_shape=(
            jax.ShapeDtypeStruct(big.shape, jnp.bfloat16),
            jax.ShapeDtypeStruct(small.shape, jnp.bfloat16),
        ),
        in_specs=[pl.BlockSpec(memory_space=pltpu.VMEM)] * 2,
        out_specs=[pl.BlockSpec(memory_space=pltpu.VMEM)] * 2,
        scratch_shapes=[
            pltpu.VMEM((rows, 128), jnp.float32),
            pltpu.VMEM((rows, 128), jnp.bfloat16),
            pltpu.VMEM((rows, 128), jnp.bfloat16),
            pltpu.VMEM((rows, 128), jnp.bfloat16),
            pltpu.SemaphoreType.DMA((len(groups), 2 * bits)),
            pltpu.SemaphoreType.DMA((len(groups), 2 * bits)),
        ],
        compiler_params=pltpu.CompilerParams(collective_id=0, has_side_effects=True),
        name="sum_over_devices",
    )(big, small)
    return tuple(part.astype(jnp.float32) for part in summed)


def local(
    features, w_hidden, w_out, items, routes, cluster_slot, sample_ids, sample_counts, positives
):
    devices = lax.axis_size("dev")
    users, visits = routes.shape
    clusters = cluster_slot.shape[0]
    local_clusters = sample_ids.shape[0]
    width = w_out.shape[1]
    item_rows = items.shape[0] // local_clusters
    capacity = max(2, 2 * users * visits // (local_clusters * devices))
    rows = local_clusters * capacity
    code, send_target = slot_codes(routes.T, positives, cluster_slot, capacity)
    seats = lax.broadcasted_iota(jnp.int32, (1, capacity, 1), 1).astype(jnp.bfloat16)
    seated = code[:, None, :] == seats
    select = seated.astype(jnp.bfloat16).reshape(clusters * capacity, users)
    send_target = send_target.reshape(capacity, devices, local_clusters)
    send_target = send_target.transpose(1, 0, 2).reshape(devices, rows)
    coded = jnp.concatenate([send_target // 64, send_target % 64], axis=1)
    extra = -(-coded.shape[1] // (8 * width)) * 8
    coded = jnp.pad(coded, ((0, 0), (0, extra * width - coded.shape[1])))
    coded = coded.astype(jnp.bfloat16).reshape(devices, extra, width)
    pre = jnp.dot(features, w_hidden, preferred_element_type=jnp.float32)
    hidden = jax.nn.silu(pre).astype(jnp.bfloat16)
    query = jnp.dot(hidden, w_out, preferred_element_type=jnp.float32).astype(jnp.bfloat16)
    send_query = jnp.dot(select, query, preferred_element_type=jnp.float32).astype(jnp.bfloat16)
    payload = jnp.concatenate([send_query.reshape(devices, rows, width), coded], axis=1)
    got = lax.all_to_all(payload, "dev", split_axis=0, concat_axis=0, tiled=True)
    got_query = got[:, :rows].reshape(devices, local_clusters, capacity, width)
    got_query = got_query.transpose(1, 0, 2, 3).reshape(local_clusters, devices * capacity, width)
    got_coded = got[:, rows:].reshape(devices, extra * width).astype(jnp.int32)
    got_target = got_coded[:, :rows] * 64 + got_coded[:, rows : 2 * rows] - 1
    got_target = got_target.reshape(devices, capacity, local_clusters)
    got_target = got_target.transpose(2, 0, 1).reshape(local_clusters, devices * capacity)
    slot_loss, dquery, dtable = owner(
        got_query,
        got_target,
        items.reshape(local_clusters, item_rows, width),
        sample_ids,
        sample_counts,
    )
    back = dquery.reshape(local_clusters, devices, capacity, width).transpose(1, 0, 2, 3)
    returned = lax.all_to_all(
        back.reshape(devices, rows, width), "dev", split_axis=0, concat_axis=0, tiled=True
    ).reshape(clusters * capacity, width)
    dq_total = lax.dot_general(
        select, returned, (((0,), (0,)), ((), ())), preferred_element_type=jnp.float32
    ).astype(jnp.bfloat16)
    local_out = jnp.dot(hidden.T, dq_total, preferred_element_type=jnp.float32)
    dhidden = jnp.dot(dq_total, w_out.T, preferred_element_type=jnp.float32)
    dpre = (dhidden * silu_grad(pre)).astype(jnp.bfloat16)
    local_hidden = jnp.dot(features.T, dpre, preferred_element_type=jnp.float32)
    grad_hidden, grad_out = sum_over_devices(local_hidden, local_out)
    return (slot_loss, grad_hidden, grad_out, dtable.reshape(items.shape[0], width))


def solution(mesh):
    in_specs = (
        P("dev", None),
        P(),
        P(),
        P("dev", None),
        P("dev", None),
        P(),
        P("dev", None),
        P("dev", None),
        P("dev", None),
    )
    out_specs = (P("dev"), P(), P(), P("dev", None))
    return jax.shard_map(local, mesh=mesh, in_specs=in_specs, out_specs=out_specs, check_vma=False)
```

profile of v0, /device:TPU:1, one launch (start us, length us, event | category | flops | bytes accessed | tf_op | source)
XLA Modules:
  0.0 131.2 jit_solution(3561932637017440707)
XLA Ops:
  0.6 0.0 copy-start
  0.7 1.4 %select_reduce_fusion.2 = s32[4,512]{1,0:T(4,128)S(1)} fusion(s32[512]{0:T(512)} %param.14, s32[4,512]{1,0:T(4,128)} %bitcast.119), kind=kLoop, calls=%fused_computation.10 | loop fusion | flops 3143680 | bytes 18432 | tf_op jit(solution)/shard_map/reduce_sum | solution.py:20
  2.1 0.9 slice_add_fusion.4
  3.0 0.2 eq.221
  3.2 1.1 convolution_select_fusion
  4.3 0.6 select_select_fusion
  4.9 0.9 select_reduce_fusion.1
  5.8 0.1 reshape.315
  5.9 0.1 copy.79
  6.0 0.1 copy.80
  6.2 3.0 %multiply_convert_fusion = (bf16[512,512]{1,0:T(8,128)(2,1)S(1)}, f32[512,512]{1,0:T(8,128)}) fusion(bf16[512,1024]{1,0:T(8,128)(2,1)S(1)} %copy-done, bf16[1024,512]{1,0:T(8,128)(2,1)} %param.10), kind=kOutput, calls=%fused_computation.66 | convolution fusion | flops 538181632 | bytes 3670016 | tf_op jit(solution)/shard_map/dot_general | solution.py:274
  9.1 0.8 fusion.18
  10.0 0.1 copy-done.16
  10.2 2.2 %fusion.5 = bf16[4096,128]{1,0:T(8,128)(2,1)S(1)} fusion(bf16[4096]{0:T(1024)(128)(2,1)S(1)} %eq.221, bf16[512,512]{1,0:T(8,128)(2,1)S(1)} %fusion.18, bf16[512,512]{1,0:T(8,128)(2,1)S(1)} %get-tuple-element.34, bf16[512,128]{1,0:T(8,128)(2,1)S(1)} %copy-done.16), kind=kOutput, calls=%fused_computation.8 | convolution fusion | flops 606666752 | bytes 2236416 | tf_op jit(solution)/shard_map/dot_general | solution.py:277
  12.3 0.0 copy-done.19
  12.3 0.0 copy-start.4
  12.3 0.0 copy-start.3
  12.4 1.1 pad_maximum_fusion
  13.4 7.1 %all-to-all-start = ((bf16[32,136,128]{2,1,0:T(8,128)(2,1)}), bf16[32,136,128]{2,1,0:T(8,128)(2,1)S(1)}, u32[]{:S(2)}, u32[]{:S(2)}) async-start(bf16[32,136,128]{2,1,0:T(8,128)(2,1)} %pad_maximum_fusion), calls=%async_computation | async-start | bytes 2228224 | tf_op jit(solution)/shard_map/all_to_all | solution.py:279
  20.6 0.0 copy-done.3
  20.6 5.3 %select_reduce_fusion = f32[16,128]{1,0:T(8,128)S(1)} fusion(f32[16,4096]{1,0:T(8,128)S(1)} %convert_divide_fusion, s32[16,4096]{1,0:T(8,128)S(1)} %copy-done.3), kind=kLoop, calls=%fused_computation | loop fusion | flops 25163776 | bytes 532480 | tf_op jit(solution)/shard_map/reduce_sum | solution.py:57
  25.9 0.2 fusion.55
  26.2 0.1 copy.107
  26.3 20.9 %all-to-all-done = bf16[32,136,128]{2,1,0:T(8,128)(2,1)S(1)} async-done(((bf16[32,136,128]{2,1,0:T(8,128)(2,1)}), bf16[32,136,128]{2,1,0:T(8,128)(2,1)S(1)}, u32[]{:S(2)}, u32[]{:S(2)}) %all-to-all-start) | async-done | bytes 1114144 | tf_op jit(solution)/shard_map/all_to_all | solution.py:279
  47.2 0.1 copy.84
  47.3 0.1 copy.87
  47.4 0.1 copy.88
  47.5 0.0 copy-start.5
  47.6 1.4 %select_reduce_fusion.5 = (f32[16,256]{1,0:T(8,128)S(1)}, f32[16,256]{1,0:T(8,128)S(1)}, f32[16,256]{1,0:T(8,128)S(1)}) fusion(s32[16,256]{1,0:T(8,128)S(1)} %broadcast_add_fusion.1, s32[16,256]{1,0:T(8,128)S(1)} %get-tuple-element.15, s32[16,256]{1,0:T(8,128)S(1)} %get-tuple-element.16, bf16[16,96,128]{2,1,0:T(8,128)(2,1)S(1)} %bitcast.102, ...), kind=kOutput, calls=%fused_computation.31 | convolution fusion | flops 104714240 | bytes 507904 | tf_op jit(solution)/shard_map/cql,chl->cqh/dot_general | solution.py:68
  49.0 0.0 copy-done.1
  49.0 0.0 copy-start.10
  49.0 0.0 copy-done.5
  49.0 1.7 %add_reduce_fusion = (f32[16,256]{1,0:T(8,128)S(1)}, f32[16,256,128]{1,2,0:T(8,128)S(1)}) fusion(f32[16,128]{1,0:T(8,128)S(1)} %log.16, bf16[16,128,128]{2,1,0:T(8,128)(2,1)S(1)} %bitcast.93, bf16[32,136,128]{2,1,0:T(8,128)(2,1)} %copy-done.1), kind=kOutput, calls=%fused_computation.26 | convolution fusion | flops 135262208 | bytes 3694592 | tf_op jit(solution)/shard_map/cqe,cie->cqi/dot_general | solution.py:77
  50.7 1.0 select_reduce_fusion.3
  51.7 0.0 copy-start.12
  51.7 1.3 fusion.52
  53.0 1.3 fusion.16
  54.3 1.3 copy.124
  55.6 4.7 %all-to-all-start.1 = ((bf16[32,128,128]{2,1,0:T(8,128)(2,1)}), bf16[32,128,128]{2,1,0:T(8,128)(2,1)}, u32[]{:S(2)}, u32[]{:S(2)}) async-start(bf16[32,128,128]{2,1,0:T(8,128)(2,1)} %bitcast.89), calls=%async_computation.1 | async-start | bytes 2097152 | tf_op jit(solution)/shard_map/all_to_all | solution.py:294
  60.3 0.1 copy.94
  60.4 0.1 copy.95
  60.5 0.0 copy-done.12
  60.5 0.1 copy.86
  60.6 0.1 copy.97
  60.7 0.1 copy.93
  60.8 0.1 copy.96
  60.9 0.2 convert_reduce_fusion
  61.1 0.5 div.73
  61.6 2.2 %fusion.23 = f32[16,128,128]{2,1,0:T(8,128)S(1)} fusion(f32[16,256,128]{1,2,0:T(8,128)S(1)} %get-tuple-element.37, f32[16,256]{1,0:T(8,128)} %copy-done.12, s32[16,256]{1,0:T(8,128)} %copy-done.10, f32[16,256]{1,0:T(8,128)S(1)} %get-tuple-element.36, f32[16,128]{1,0:T(8,128)} %copy-done.8, bf16[32,136,128]{2,1,0:T(8,128)(2,1)} %copy-done.1), kind=kOutput, calls=%fused_computation.47 | convolution fusion | flops 138412032 | bytes 4251648 | tf_op jit(solution)/shard_map/cqi,cqe->cie/dot_general | solution.py:97
  63.8 0.0 copy-done.2
  63.8 0.0 copy-done.9
  63.9 0.0 copy-done.11
  63.9 0.0 copy-done.13
  63.9 0.0 copy-start.15
  63.9 2.0 %convolution_add_fusion = f32[16,128,128]{2,1,0:T(8,128)} fusion(f32[16,128,128]{2,1,0:T(8,128)S(1)} %fusion.23, f32[16,256,128]{1,2,0:T(8,128)S(1)} %get-tuple-element.37, f32[16,256]{1,0:T(8,128)S(1)} %copy-done.13, s32[16,256]{1,0:T(8,128)S(1)} %copy-done.11, f32[16,256]{1,0:T(8,128)S(1)} %get-tuple-element.36, f32[16,128]{1,0:T(8,128)S(1)} %copy-done.9, ...), kind=kOutput, calls=%fused_computation.38 | convolution fusion | flops 139198464 | bytes 5300224 | tf_op jit(solution)/shard_map/cqi,cqe->cie/dot_general | solution.py:99
  65.9 19.6 %all-to-all-done.1 = bf16[32,128,128]{2,1,0:T(8,128)(2,1)} async-done(((bf16[32,128,128]{2,1,0:T(8,128)(2,1)}), bf16[32,128,128]{2,1,0:T(8,128)(2,1)}, u32[]{:S(2)}, u32[]{:S(2)}) %all-to-all-start.1) | async-done | bytes 1048608 | tf_op jit(solution)/shard_map/all_to_all | solution.py:294
  85.5 4.0 %fusion.19 = bf16[512,128]{1,0:T(8,128)(2,1)S(1)} fusion(bf16[4096,128]{1,0:T(8,128)(2,1)} %bitcast.33, bf16[512,512]{1,0:T(8,128)(2,1)} %copy-done.19, bf16[8]{0:T(256)(128)(2,1)S(1)} %copy-done.15), kind=kOutput, calls=%fused_computation.43 | convolution fusion | flops 539033600 | bytes 1703952 | tf_op jit(solution)/shard_map/dot_general | solution.py:297
  89.5 0.0 copy-done.7
  89.5 1.0 fusion.73.small_ref
  90.5 0.0 copy-done.18
  90.5 2.3 %convolution_bitcast_fusion.big_ref = f32[1024,512]{1,0:T(8,128)} fusion(bf16[512,1024]{1,0:T(8,128)(2,1)S(1)} %copy-done, bf16[512,128]{1,0:T(8,128)(2,1)S(1)} %fusion.19, bf16[512,128]{1,0:T(8,128)(2,1)S(1)} %copy-done.17, f32[512,512]{1,0:T(8,128)S(1)} %copy-done.18), kind=kOutput, calls=%fused_computation.28 | convolution fusion | flops 606339072 | bytes 4456448 | tf_op jit(solution)/shard_map/dot_general | solution.py:303
  92.9 33.9 %sum_over_devices.1 = (bf16[1024,512]{1,0:T(8,128)(2,1)}, bf16[512,128]{1,0:T(8,128)(2,1)}) custom-call(f32[1024,512]{1,0:T(8,128)} %convolution_bitcast_fusion.big_ref, f32[512,128]{1,0:T(8,128)} %fusion.73.small_ref), custom_call_target="tpu_custom_call" | custom-call | tf_op jit(solution)/shard_map/sum_over_devices/pallas_call | solution.py:231
  126.8 1.6 %convert_element_type.104 = f32[512,128]{1,0:T(8,128)} convert(bf16[512,128]{1,0:T(8,128)(2,1)} %get-tuple-element.7) | non-fusion elementwise | flops 65536 | bytes 393216 | tf_op jit(solution)/shard_map/convert_element_type | solution.py:250
  128.4 2.8 %convert_element_type.103 = f32[1024,512]{1,0:T(8,128)} convert(bf16[1024,512]{1,0:T(8,128)(2,1)} %get-tuple-element.6) | non-fusion elementwise | flops 524288 | bytes 3145728 | tf_op jit(solution)/shard_map/convert_element_type | solution.py:250
  (41 shorter events, 0.4 us)
Async XLA Ops:
  0.6 5.5 %copy-start = (bf16[512,1024]{1,0:T(8,128)(2,1)S(1)}, bf16[512,1024]{1,0:T(8,128)(2,1)}, u32[]{:S(2)}) copy-start(bf16[512,1024]{1,0:T(8,128)(2,1)} %param.9) | copy-start | bytes 3145732
  0.7 3.6 %copy-start.14 = (bf16[8]{0:T(256)(128)(2,1)}, bf16[8]{0:T(256)(128)(2,1)S(1)}, u32[]{:S(2)}) copy-start(bf16[8]{0:T(256)(128)(2,1)S(1)} %iota_convert_fusion.1) | copy-start | bytes 52
  9.1 0.9 copy-start.6
  9.1 1.0 copy-start.16
  10.0 2.3 %copy-start.19 = (bf16[512,512]{1,0:T(8,128)(2,1)}, bf16[512,512]{1,0:T(8,128)(2,1)S(1)}, u32[]{:S(2)}) copy-start(bf16[512,512]{1,0:T(8,128)(2,1)S(1)} %fusion.18) | copy-start | bytes 1572868
  12.3 8.2 %copy-start.4 = (s32[16,4096]{1,0:T(8,128)S(1)}, s32[16,4096]{1,0:T(8,128)}, u32[]{:S(2)}) copy-start(s32[16,4096]{1,0:T(8,128)} %param.16) | copy-start | bytes 786436
  12.3 8.3 %copy-start.3 = (s32[16,4096]{1,0:T(8,128)S(1)}, s32[16,4096]{1,0:T(8,128)}, u32[]{:S(2)}) copy-start(s32[16,4096]{1,0:T(8,128)} %param.15) | copy-start | bytes 786436
  13.4 33.7 %all-to-all-start = ((bf16[32,136,128]{2,1,0:T(8,128)(2,1)}), bf16[32,136,128]{2,1,0:T(8,128)(2,1)S(1)}, u32[]{:S(2)}, u32[]{:S(2)}) async-start(bf16[32,136,128]{2,1,0:T(8,128)(2,1)} %pad_maximum_fusion), calls=%async_computation | async-start | bytes 2228224 | tf_op jit(solution)/shard_map/all_to_all | solution.py:279
  25.9 27.1 %copy-start.8 = (f32[16,128]{1,0:T(8,128)}, f32[16,128]{1,0:T(8,128)S(1)}, u32[]{:S(2)}) copy-start(f32[16,128]{1,0:T(8,128)S(1)} %log.16) | copy-start | bytes 24580
  47.1 1.8 %copy-start.1 = (bf16[32,136,128]{2,1,0:T(8,128)(2,1)}, bf16[32,136,128]{2,1,0:T(8,128)(2,1)S(1)}, u32[]{:S(2)}) copy-start(bf16[32,136,128]{2,1,0:T(8,128)(2,1)S(1)} %all-to-all-done) | copy-start | bytes 3342340
  47.5 1.5 %copy-start.5 = (bf16[2048,128]{1,0:T(8,128)(2,1)S(1)}, bf16[2048,128]{1,0:T(8,128)(2,1)}, u32[]{:S(2)}) copy-start(bf16[2048,128]{1,0:T(8,128)(2,1)} %param.12) | copy-start | bytes 1572868
  49.0 4.0 %copy-start.10 = (s32[16,256]{1,0:T(8,128)}, s32[16,256]{1,0:T(8,128)S(1)}, u32[]{:S(2)}) copy-start(s32[16,256]{1,0:T(8,128)S(1)} %convert_select_fusion) | copy-start | bytes 49156
  51.7 8.8 %copy-start.12 = (f32[16,256]{1,0:T(8,128)}, f32[16,256]{1,0:T(8,128)S(1)}, u32[]{:S(2)}) copy-start(f32[16,256]{1,0:T(8,128)S(1)} %get-tuple-element.9) | copy-start | bytes 49156
  55.6 29.9 %all-to-all-start.1 = ((bf16[32,128,128]{2,1,0:T(8,128)(2,1)}), bf16[32,128,128]{2,1,0:T(8,128)(2,1)}, u32[]{:S(2)}, u32[]{:S(2)}) async-start(bf16[32,128,128]{2,1,0:T(8,128)(2,1)} %bitcast.89), calls=%async_computation.1 | async-start | bytes 2097152 | tf_op jit(solution)/shard_map/all_to_all | solution.py:294
  61.6 2.2 %copy-start.2 = (bf16[32,136,128]{2,1,0:T(8,128)(2,1)S(1)}, bf16[32,136,128]{2,1,0:T(8,128)(2,1)}, u32[]{:S(2)}) copy-start(bf16[32,136,128]{2,1,0:T(8,128)(2,1)} %copy-done.1) | copy-start | bytes 3342340
  61.6 2.3 %copy-start.9 = (f32[16,128]{1,0:T(8,128)S(1)}, f32[16,128]{1,0:T(8,128)}, u32[]{:S(2)}) copy-start(f32[16,128]{1,0:T(8,128)} %copy-done.8) | copy-start | bytes 24580
  61.6 2.3 %copy-start.11 = (s32[16,256]{1,0:T(8,128)S(1)}, s32[16,256]{1,0:T(8,128)}, u32[]{:S(2)}) copy-start(s32[16,256]{1,0:T(8,128)} %copy-done.10) | copy-start | bytes 49156
  61.6 2.3 %copy-start.13 = (f32[16,256]{1,0:T(8,128)S(1)}, f32[16,256]{1,0:T(8,128)}, u32[]{:S(2)}) copy-start(f32[16,256]{1,0:T(8,128)} %copy-done.12) | copy-start | bytes 49156
  63.9 21.6 %copy-start.15 = (bf16[8]{0:T(256)(128)(2,1)S(1)}, bf16[8]{0:T(256)(128)(2,1)}, u32[]{:S(2)}) copy-start(bf16[8]{0:T(256)(128)(2,1)} %copy-done.14) | copy-start | bytes 52
  85.5 4.0 %copy-start.7 = (bf16[512,512]{1,0:T(8,128)(2,1)S(1)}, bf16[512,512]{1,0:T(8,128)(2,1)}, u32[]{:S(2)}) copy-start(bf16[512,512]{1,0:T(8,128)(2,1)} %copy-done.6) | copy-start | bytes 1572868
  85.5 5.0 %copy-start.17 = (bf16[512,128]{1,0:T(8,128)(2,1)S(1)}, bf16[512,128]{1,0:T(8,128)(2,1)}, u32[]{:S(2)}) copy-start(bf16[512,128]{1,0:T(8,128)(2,1)} %param.11) | copy-start | bytes 393220
  85.5 5.0 %copy-start.18 = (f32[512,512]{1,0:T(8,128)S(1)}, f32[512,512]{1,0:T(8,128)}, u32[]{:S(2)}) copy-start(f32[512,512]{1,0:T(8,128)} %get-tuple-element.35) | copy-start | bytes 3145732
where the time goes:
time: 132 us; the launch traced here: 131 us
  waiting for transfers between devices  40.4 us (31%)
  Pallas kernels  33.9 us (26%)
  matrix products  24.3 us (18%)
  other arithmetic  16.7 us (13%)
  starting transfers between devices  11.8 us (9%)
  local copies, waits for them, and re-layouts  2.94 us (2%)
    pallas_call x1, Pallas kernels, sum_over_devices(): pl.pallas_call(functools.partial(reduce_kernel, bits, tiles), out_shape=(...  33.9 us
    all_to_all x1, waiting for transfers between devices, local(): lax.all_to_all(payload, 'dev', split_axis=0, concat_axis=0, tiled=True)  20.9 us
    all_to_all x1, waiting for transfers between devices, local(): lax.all_to_all(back.reshape(devices, rows, width), 'dev', split_axis=0, c...  19.6 us
    all_to_all x1, starting transfers between devices, local(): lax.all_to_all(payload, 'dev', split_axis=0, concat_axis=0, tiled=True)  7.09 us
    reduce_sum x1, other arithmetic, owner(): jnp.sum(jnp.where(table_ids[:, None, :] == which, recip[:, None, :], 0.0)...  5.26 us
    all_to_all x1, starting transfers between devices, local(): lax.all_to_all(back.reshape(devices, rows, width), 'dev', split_axis=0, c...  4.68 us
    convert_element_type x2, other arithmetic, sum_over_devices(): return tuple((part.astype(jnp.float32) for part in summed))  4.46 us
    dot_general x1, matrix products, local(): lax.dot_general(select, returned, (((0,), (0,)), ((), ())), preferred_ele...  3.97 us
  transfers between devices with their start and end apart: 2, of which 2 were waited for; matrix products, arithmetic and copies ran while one was open for 9% of the time, Pallas kernels for 0%

commit v1 on v0

v1 whole, which is shorter than its diff:
```python
import functools

import jax
import jax.numpy as jnp
from jax import lax
from jax.experimental import pallas as pl
from jax.experimental.pallas import tpu as pltpu
from jax.sharding import PartitionSpec as P

LINE = 4
LANES = 128
TILE = 8
MESH = pl.DeviceIdType.MESH
F32, BF16, I32 = jnp.float32, jnp.bfloat16, jnp.int32
VMEM_BYTES = 67_000_000


def iota(shape, axis):
    return lax.broadcasted_iota(I32, shape, axis)


def flags(test):
    return jnp.where(test, 1.0, 0.0).astype(BF16)


def log2(value):
    return value.bit_length() - 1


def flip(index, other, size):
    result = index
    weight = 1
    while weight < size:
        mine = (index // weight) % 2
        theirs = (other // weight) % 2
        result = result + weight * (theirs - 2 * mine * theirs)
        weight *= 2
    return result


def each(low, high, action):
    def body(i, carry):
        action(i)
        return carry

    lax.fori_loop(low, high, body, 0)


def remote(src, dst, sems, at, device):
    return pltpu.make_async_remote_copy(
        src_ref=src,
        dst_ref=dst,
        send_sem=sems.at[(0,) + at],
        recv_sem=sems.at[(1,) + at],
        device_id=(device,),
        device_id_type=MESH,
    )


def split(devices, elements):
    unit = devices * TILE
    units = -(-(elements // LANES) // unit)
    first = min(units - 1, max(1, (units * 7 + 4) // 9)) if units > 1 else 1
    return units, first


def step_kernel(
    line,
    plane,
    cap,
    features_hbm,
    w_hidden_hbm,
    w_out_hbm,
    items_hbm,
    ids_hbm,
    counts_hbm,
    routes_hbm,
    spots_hbm,
    slot_hbm,
    loss_out,
    big_out,
    small_out,
    table_out,
    features,
    features_t,
    w_hidden,
    w_out,
    items,
    ids,
    counts,
    routes_ref,
    spots_ref,
    slot_ref,
    slope,
    hidden,
    metas,
    qline,
    earlier,
    codes,
    sel,
    stage,
    got,
    zstage,
    zgot,
    lookup,
    mass,
    tpos,
    wts,
    dqs,
    ret,
    pstage,
    part,
    acc,
    outb,
    core_in,
    a1_in,
    a2_in,
    b1_in,
    b2_in,
    full,
    load_sem,
    m_sem,
    q_sem,
    x_sem,
    t_sem,
    r_sem,
    p_sem,
    c_sem,
    a1_sem,
    a2_sem,
    b1_sem,
    b2_sem,
    az_sem,
    ac_sem,
    ao_sem,
    bz_sem,
    bc_sem,
    bo_sem,
):
    me = lax.axis_index("dev")
    z, p = me // plane, me % plane

    def along(j):
        return flip(z, j, line) * plane + p

    def inside(i):
        return z * plane + flip(p, i, plane)

    visits, users = routes_ref.shape
    clusters = slot_ref.shape[1]
    local_clusters, samples = ids.shape
    item_rows, width = items.shape[1:]
    rows = local_clusters * cap
    hosted = plane * local_clusters
    seats = line * plane * cap
    groups = samples // LANES

    loads = [
        pltpu.make_async_copy(src, dst, load_sem.at[n])
        for n, (src, dst) in enumerate(
            [
                (slot_hbm, slot_ref),
                (routes_hbm, routes_ref),
                (spots_hbm, spots_ref),
                (features_hbm, features),
                (w_hidden_hbm, w_hidden),
                (w_out_hbm, w_out),
                (ids_hbm, ids),
                (counts_hbm, counts),
                (items_hbm, items),
            ]
        )
    ]
    for load in loads:
        load.start()

    barrier = pltpu.get_barrier_semaphore()
    for j in range(1, line):
        pl.semaphore_signal(barrier, inc=1, device_id=(along(j),), device_id_type=MESH)
    each(
        1,
        plane,
        lambda i: pl.semaphore_signal(
            barrier, inc=1, device_id=(inside(i),), device_id_type=MESH
        ),
    )

    earlier[...] = flags(iota((users, users), 0) < iota((users, users), 1))
    for load in loads[:3]:
        load.wait()
    k = iota((hosted, 1), 0)
    host = lax.bitwise_xor(lax.shift_right_logical(k, log2(local_clusters)), p)
    slot = (z * plane + host) * local_clusters + (k & (local_clusters - 1))
    names = jnp.sum(
        jnp.where(slot_ref[...] == slot, iota((hosted, clusters), 1), 0).astype(F32),
        axis=1,
        keepdims=True,
    ).astype(I32)

    pl.semaphore_wait(barrier, line + plane - 2)

    def meta_copies(j):
        return [
            remote(src, metas.at[n, j], m_sem, (n, j), along(j))
            for n, src in enumerate((routes_ref, spots_ref))
        ]

    def query_copy(j):
        return remote(qline.at[0], qline.at[j], q_sem, (j,), along(j))

    def seat_copy(j, i):
        return remote(stage.at[j, i], got.at[:, j * plane + i], x_sem, (j, i), inside(i))

    def target_copy(i):
        return remote(zstage.at[i], zgot.at[i], t_sem, (i,), inside(i))

    def back_copy(j, i):
        return remote(dqs.at[:, j * plane + i], ret.at[j, i], r_sem, (j, i), inside(i))

    def part_copy(j):
        return remote(pstage.at[j], part.at[j], p_sem, (j,), along(j))

    for j in range(1, line):
        for copy in meta_copies(j):
            copy.start()

    for load in loads[3:6]:
        load.wait()
    pre = jnp.dot(features[...], w_hidden[...], preferred_element_type=F32)
    gate = 1.0 / (1.0 + jnp.exp(-pre))
    hidden[...] = (pre * gate).astype(BF16)
    slope[...] = gate * (1.0 + pre * (1.0 - gate))
    qline[0] = jnp.dot(hidden[...], w_out[...], preferred_element_type=F32).astype(BF16)
    for j in range(1, line):
        query_copy(j).start()

    lane = iota((1, LANES), 1)
    zstage[...] = jnp.zeros(zstage.shape, F32)

    def choose(j):
        routes = routes_ref if j == 0 else metas.at[0, j]
        spots = spots_ref if j == 0 else metas.at[1, j]
        target = jnp.zeros((hosted, users), F32)
        for r in range(visits):
            same = names == routes[r : r + 1, :]
            target = jnp.where(same, (spots[r : r + 1, :] + 1).astype(F32), target)
        member = target > 0.0
        rank = jnp.dot(flags(member), earlier[...], preferred_element_type=F32)
        code = jnp.where(member, rank, -1.0)
        codes[...] = code
        found = zstage[...].reshape(hosted, LANES)
        for s in range(cap):
            spot = jnp.sum(jnp.where(code == float(s), target, 0.0), axis=1, keepdims=True)
            found = jnp.where(lane == j * cap + s, spot, found)
        zstage[...] = found.reshape(plane, local_clusters, LANES)

        def block(i):
            own = codes[pl.ds(pl.multiple_of(i * local_clusters, TILE), local_clusters), :]
            if cap % TILE == 0:
                seat = iota((1, cap, 1), 1).astype(F32)
                chosen = flags((own[:, None, :] == seat).reshape(rows, users))
            else:
                first = iota((rows, local_clusters), 1) * cap
                row = iota((rows, local_clusters), 0)
                spread = flags((row >= first) & (row < first + cap))
                seat = (iota((rows, 1), 0) & (cap - 1)).astype(F32)
                wide = jnp.dot(spread, own.astype(BF16), preferred_element_type=F32)
                chosen = flags(wide == seat)
            sel[j, i] = chosen

        each(0, plane, block)

    def seated(j, i):
        value = jnp.dot(sel[j, i], qline[j], preferred_element_type=F32)
        return value.reshape(local_clusters, cap, width).astype(BF16)

    def send_seats(j):
        def block(i):
            stage[j, i] = seated(j, i)
            seat_copy(j, i).start()

        each(1, plane, block)
        got[:, j * plane] = seated(j, 0)

    choose(0)
    send_seats(0)
    for j in range(1, line):
        for copy in meta_copies(j):
            copy.wait_recv()
        choose(j)
    each(1, plane, lambda i: target_copy(i).start())
    zgot[0] = zstage[0]
    for j in range(1, line - 1):
        query_copy(j).wait_recv()
        send_seats(j)

    for load in loads[6:]:
        load.wait()
    for t in range(groups):
        here = slice(t * LANES, (t + 1) * LANES)
        count = counts[:, here]
        high = lax.shift_right_logical(count, 6)
        lookup[:, t, :] = ids[:, here].astype(F32)
        lookup[:, groups + t, :] = high.astype(F32)
        lookup[:, 2 * groups + t, :] = (count & 63).astype(F32)

    item = iota((item_rows, LANES), 0)
    step = 4
    for c in range(local_clusters):

        def weigh(t, total):
            for u in range(step):
                here = pl.ds(pl.multiple_of((t * step + u) * LANES, LANES), LANES)
                weight = 1.0 / counts[c : c + 1, here].astype(F32)
                total = total + jnp.where(ids[c : c + 1, here] == item, weight, 0.0)
            return total

        total = lax.fori_loop(0, groups // step, weigh, jnp.zeros((item_rows, LANES), F32))
        mass[c] = jnp.log(jnp.sum(total, axis=1, keepdims=True))

    query_copy(line - 1).wait_recv()
    send_seats(line - 1)

    features_t[...] = features[...].T
    each(1, plane, lambda i: target_copy(i).wait_recv())

    entry = iota((LANES, seats), 0)
    column = iota((LANES, seats), 1)
    source = lax.shift_right_logical(column, log2(cap))
    place = lax.shift_right_logical(source, log2(plane)) * cap + (column & (cap - 1))
    widen = flags(entry == place)
    from_row = lax.shift_right_logical(iota((hosted, seats), 0), log2(local_clusters))
    from_column = lax.shift_right_logical(iota((hosted, seats), 1), log2(cap)) & (plane - 1)
    matched = from_row == from_column
    fold = flags(
        iota((local_clusters, hosted), 0)
        == (iota((local_clusters, hosted), 1) & (local_clusters - 1))
    )
    z_all = zgot[...].reshape(hosted, LANES)
    z_high = jnp.floor(z_all * (1.0 / 64.0))
    z_low = z_all - z_high * 64.0

    def regroup(value):
        spread = jnp.dot(value.astype(BF16), widen, preferred_element_type=F32)
        spread = jnp.where(matched, spread, 0.0).astype(BF16)
        return jnp.dot(fold, spread, preferred_element_type=F32)

    spots_all = (regroup(z_high) * 64.0 + regroup(z_low)).astype(I32)
    for c in range(local_clusters):
        tpos[c] = spots_all[c : c + 1, :]

    for j in range(line):
        each(1, plane, lambda i: seat_copy(j, i).wait_recv())

    item_wide = iota((item_rows, seats), 0)
    low_wide = iota((LANES, seats), 0)
    high_wide = iota((groups, seats), 0)
    loss_lane = iota((1, loss_out.shape[1]), 1)

    def own(c, losses):
        query = got[c].reshape(seats, width)
        block = items[c]
        scores = lax.dot_general(
            block, query, (((1,), (1,)), ((), ())), preferred_element_type=F32
        )
        shifted = scores + mass[c]
        top = jnp.max(shifted, axis=0, keepdims=True)
        expo = jnp.exp(shifted - top)
        total = jnp.sum(expo, axis=0, keepdims=True)
        spot = tpos[c] - 1
        live = spot >= 0
        near = jnp.dot(
            lookup[c].astype(BF16),
            flags((spot & (LANES - 1)) == low_wide),
            preferred_element_type=F32,
        )
        here = lax.shift_right_logical(spot, log2(LANES)) == high_wide
        found = [
            jnp.sum(
                jnp.where(here, near[n * groups : (n + 1) * groups, :], 0.0), axis=0, keepdims=True
            )
            for n in range(3)
        ]
        own_id = jnp.where(live, found[0], -1.0).astype(I32)
        own_count = jnp.where(live, found[1] * 64.0 + found[2], 1.0)
        hit = own_id == item_wide
        picked = jnp.sum(jnp.where(hit, scores, 0.0), axis=0, keepdims=True) - jnp.log(own_count)
        loss = jnp.where(live, jnp.log(total) + top - picked, 0.0)
        mean = jnp.sum(loss, axis=1, keepdims=True) / jnp.sum(
            jnp.where(live, 1.0, 0.0), axis=1, keepdims=True
        )
        weight = (expo * (1.0 / total) - jnp.where(hit, 1.0, 0.0)).astype(BF16)
        wts[c] = weight
        dq = lax.dot_general(weight, block, (((0,), (0,)), ((), ())), preferred_element_type=F32)
        dqs[c] = dq.reshape(line * plane, cap, width).astype(BF16)
        return jnp.where(loss_lane == c, mean, losses)

    loss_out[...] = lax.fori_loop(0, local_clusters, own, jnp.zeros(loss_out.shape, F32))

    for j in range(line - 1, -1, -1):
        each(1, plane, lambda i: back_copy(j, i).start())
        ret[j, 0] = dqs[:, j * plane]

    def tables(c):
        table_out[c] = jnp.dot(
            wts[c], got[c].reshape(seats, width), preferred_element_type=F32
        )

    each(0, local_clusters, tables)

    def gather(j):
        each(1, plane, lambda i: back_copy(j, i).wait_recv())
        return lax.dot_general(
            sel[j].reshape(plane * rows, users),
            ret[j].reshape(plane * rows, width),
            (((0,), (0,)), ((), ())),
            preferred_element_type=F32,
        )

    for j in range(line - 1, 0, -1):
        pstage[j] = gather(j).astype(BF16)
        part_copy(j).start()
    total = gather(0)
    for j in range(1, line):
        part_copy(j).wait_recv()
        total = total + part[j].astype(F32)
    dq_total = total.astype(BF16)

    feat, hid = features.shape[1], hidden.shape[1]
    dhidden = lax.dot_general(
        dq_total, w_out[...], (((1,), (1,)), ((), ())), preferred_element_type=F32
    )
    dpre = (dhidden * slope[...]).astype(BF16)
    wide = 2 * LANES
    for b in range(hid // wide):
        product = jnp.dot(
            features_t[...], dpre[:, b * wide : (b + 1) * wide], preferred_element_type=F32
        )
        for h in range(2):
            acc[(2 * b + h) * feat : (2 * b + h + 1) * feat, :] = product[
                :, h * LANES : (h + 1) * LANES
            ]
    big_rows = feat * (hid // LANES)
    acc[big_rows : big_rows + hid, :] = lax.dot_general(
        hidden[...], dq_total, (((0,), (0,)), ((), ())), preferred_element_type=F32
    )
    if acc.shape[0] > big_rows + hid:
        spare = acc.shape[0] - big_rows - hid
        acc[big_rows + hid :, :] = jnp.zeros((spare, LANES), F32)

    chips = plane // 2
    core, chip = p % 2, p // 2
    units, a_units = split(line * plane, (feat + width) * hid)
    parts = line * chips * TILE
    a_len, b_len = a_units * parts, (units - a_units) * parts
    half = a_len + b_len
    a1_len, b1_len = a_len // chips, b_len // line
    a2_len, b2_len = a1_len // line, b1_len // chips
    base = core * half
    away = (1 - core) * half

    def at(start, size):
        return pl.ds(pl.multiple_of(start, TILE), size)

    def a_block(i):
        return base + flip(chip, i, chips) * a1_len

    def a_piece(i, j):
        return a_block(i) + flip(z, j, line) * a2_len

    def b_block(j):
        return base + a_len + flip(z, j, line) * b1_len

    def b_piece(j, i):
        return b_block(j) + flip(chip, i, chips) * b2_len

    started = []

    def give(start, size, inbox, sems, index, device):
        span = at(start, size)
        outb[span, :] = acc[span, :].astype(BF16)
        copy = remote(outb.at[span, :], inbox, sems, index, device)
        copy.start()
        started.append(copy)
        return copy

    def add(start, size, *arrived):
        span = at(start, size)
        total = acc[span, :]
        for inbox in arrived:
            total = total + inbox.astype(F32)
        acc[span, :] = total

    def chip_at(i):
        return inside(2 * i)

    core_a = give(away, a_len, core_in.at[0:a_len, :], c_sem, (0,), inside(1))
    core_b = give(away + a_len, b_len, core_in.at[a_len:half, :], c_sem, (1,), inside(1))
    core_a.wait_recv()
    add(base, a_len, core_in[0:a_len, :])
    a1 = [give(a_block(i), a1_len, a1_in.at[i], a1_sem, (i,), chip_at(i)) for i in range(1, chips)]
    core_b.wait_recv()
    add(base + a_len, b_len, core_in[a_len:half, :])
    b1 = [give(b_block(j), b1_len, b1_in.at[j], b1_sem, (j,), along(j)) for j in range(1, line)]
    for copy in a1:
        copy.wait_recv()
    add(a_block(0), a1_len, *[a1_in[i] for i in range(1, chips)])
    a2 = [give(a_piece(0, j), a2_len, a2_in.at[j], a2_sem, (j,), along(j)) for j in range(1, line)]
    for copy in b1:
        copy.wait_recv()
    add(b_block(0), b1_len, *[b1_in[j] for j in range(1, line)])
    b2 = [
        give(b_piece(0, i), b2_len, b2_in.at[i], b2_sem, (i,), chip_at(i)) for i in range(1, chips)
    ]

    def share(start, size, sems, index, device):
        span = at(start, size)
        copy = remote(full.at[span, :], full.at[span, :], sems, index, device)
        copy.start()
        started.append(copy)
        return copy

    def settle(start, size, *arrived):
        span = at(start, size)
        total = acc[span, :]
        for inbox in arrived:
            total = total + inbox.astype(F32)
        full[span, :] = total.astype(BF16)

    for copy in a2:
        copy.wait_recv()
    settle(a_piece(0, 0), a2_len, *[a2_in[j] for j in range(1, line)])
    az = [share(a_piece(0, 0), a2_len, az_sem, (j,), along(j)) for j in range(1, line)]
    ac = {}
    for i in range(1, chips):
        ac[i, 0] = share(a_piece(0, 0), a2_len, ac_sem, (i, 0), chip_at(i))
    for copy in b2:
        copy.wait_recv()
    settle(b_piece(0, 0), b2_len, *[b2_in[i] for i in range(1, chips)])
    bc = [share(b_piece(0, 0), b2_len, bc_sem, (i,), chip_at(i)) for i in range(1, chips)]
    bz = {}
    for j in range(1, line):
        bz[j, 0] = share(b_piece(0, 0), b2_len, bz_sem, (j, 0), along(j))
    for j in range(1, line):
        az[j - 1].wait_recv()
        for i in range(1, chips):
            ac[i, j] = share(a_piece(0, j), a2_len, ac_sem, (i, j), chip_at(i))
    ao = [share(a_block(0), a1_len, ao_sem, (0,), inside(1))]
    for i in range(1, chips):
        bc[i - 1].wait_recv()
        for j in range(1, line):
            bz[j, i] = share(b_piece(0, i), b2_len, bz_sem, (j, i), along(j))
    bo = [share(b_block(0), b1_len, bo_sem, (0,), inside(1))]
    for j in range(1, line):
        for i in range(chips):
            bz[j, i].wait_recv()
        bo.append(share(b_block(j), b1_len, bo_sem, (j,), inside(1)))
    for i in range(1, chips):
        for j in range(line):
            ac[i, j].wait_recv()
        ao.append(share(a_block(i), a1_len, ao_sem, (i,), inside(1)))
    for copy in ao + bo:
        copy.wait_recv()
    for b in range(hid // LANES):
        big_out[:, b * LANES : (b + 1) * LANES] = full[b * feat : (b + 1) * feat, :].astype(
            big_out.dtype
        )
    small_out[...] = full[big_rows : big_rows + hid, :].astype(small_out.dtype)

    for copy in started:
        copy.wait_send()
    for j in range(1, line):
        for copy in meta_copies(j) + [query_copy(j), part_copy(j)]:
            copy.wait_send()

    def sent(i):
        target_copy(i).wait_send()
        for j in range(line):
            seat_copy(j, i).wait_send()
            back_copy(j, i).wait_send()

    each(1, plane, sent)


def local(
    features, w_hidden, w_out, items, routes, cluster_slot, sample_ids, sample_counts, positives
):
    devices = lax.axis_size("dev")
    line, plane = LINE, devices // LINE
    chips = plane // 2
    users, visits = routes.shape
    feat, hid = w_hidden.shape
    width = w_out.shape[1]
    clusters = cluster_slot.shape[0]
    local_clusters, samples = sample_ids.shape
    item_rows = items.shape[0] // local_clusters
    cap = max(2, 2 * users * visits // (local_clusters * devices))
    rows = local_clusters * cap
    hosted = plane * local_clusters
    seats = devices * cap
    groups = samples // LANES
    units, a_units = split(devices, (feat + width) * hid)
    parts = line * chips * TILE
    a_len, b_len = a_units * parts, (units - a_units) * parts
    half = a_len + b_len
    vmem = pl.BlockSpec(memory_space=pltpu.VMEM)
    hbm = pl.BlockSpec(memory_space=pltpu.HBM)
    dma = pltpu.SemaphoreType.DMA
    loss, big, small, table = pl.pallas_call(
        functools.partial(step_kernel, line, plane, cap),
        out_shape=(
            jax.ShapeDtypeStruct((1, local_clusters), F32),
            jax.ShapeDtypeStruct((feat, hid), OUT),
            jax.ShapeDtypeStruct((hid, width), OUT),
            jax.ShapeDtypeStruct((local_clusters, item_rows, width), F32),
        ),
        in_specs=[hbm] * 9,
        out_specs=[vmem] * 4,
        scratch_shapes=[
            pltpu.VMEM((users, feat), BF16),
            pltpu.VMEM((feat, users), BF16),
            pltpu.VMEM((feat, hid), BF16),
            pltpu.VMEM((hid, width), BF16),
            pltpu.VMEM((local_clusters, item_rows, width), BF16),
            pltpu.VMEM((local_clusters, samples), I32),
            pltpu.VMEM((local_clusters, samples), I32),
            pltpu.VMEM((visits, users), I32),
            pltpu.VMEM((visits, users), I32),
            pltpu.VMEM((1, clusters), I32),
            pltpu.VMEM((users, hid), F32),
            pltpu.VMEM((users, hid), BF16),
            pltpu.VMEM((2, line, visits, users), I32),
            pltpu.VMEM((line, users, width), BF16),
            pltpu.VMEM((users, users), BF16),
            pltpu.VMEM((hosted, users), F32),
            pltpu.VMEM((line, plane, rows, users), BF16),
            pltpu.VMEM((line, plane, local_clusters, cap, width), BF16),
            pltpu.VMEM((local_clusters, devices, cap, width), BF16),
            pltpu.VMEM((plane, local_clusters, LANES), F32),
            pltpu.VMEM((plane, local_clusters, LANES), F32),
            pltpu.VMEM((local_clusters, 3 * groups, LANES), F32),
            pltpu.VMEM((local_clusters, item_rows, 1), F32),
            pltpu.VMEM((local_clusters, 1, seats), I32),
            pltpu.VMEM((local_clusters, item_rows, seats), BF16),
            pltpu.VMEM((local_clusters, devices, cap, width), BF16),
            pltpu.VMEM((line, plane, local_clusters, cap, width), BF16),
            pltpu.VMEM((line, users, width), BF16),
            pltpu.VMEM((line, users, width), BF16),
            pltpu.VMEM((2 * half, LANES), F32),
            pltpu.VMEM((2 * half, LANES), BF16),
            pltpu.VMEM((half, LANES), BF16),
            pltpu.VMEM((chips, a_len // chips, LANES), BF16),
            pltpu.VMEM((line, a_len // chips // line, LANES), BF16),
            pltpu.VMEM((line, b_len // line, LANES), BF16),
            pltpu.VMEM((chips, b_len // line // chips, LANES), BF16),
            pltpu.VMEM((2 * half, LANES), BF16),
            dma((9,)),
            dma((2, 2, line)),
            dma((2, line)),
            dma((2, line, plane)),
            dma((2, plane)),
            dma((2, line, plane)),
            dma((2, line)),
            dma((2, 2)),
            dma((2, chips)),
            dma((2, line)),
            dma((2, line)),
            dma((2, chips)),
            dma((2, line)),
            dma((2, chips, line)),
            dma((2, chips)),
            dma((2, line, chips)),
            dma((2, chips)),
            dma((2, line)),
        ],
        compiler_params=pltpu.CompilerParams(
            collective_id=0, has_side_effects=True, vmem_limit_bytes=VMEM_BYTES
        ),
        name="step",
    )(
        features,
        w_hidden,
        w_out,
        items.reshape(local_clusters, item_rows, width),
        sample_ids,
        sample_counts,
        routes.T,
        positives.T,
        cluster_slot.reshape(1, clusters),
    )
    return (
        loss.reshape(local_clusters),
        big.astype(F32),
        small.astype(F32),
        table.reshape(items.shape),
    )


OUT = BF16


def solution(mesh):
    in_specs = (
        P("dev", None),
        P(),
        P(),
        P("dev", None),
        P("dev", None),
        P(),
        P("dev", None),
        P("dev", None),
        P("dev", None),
    )
    out_specs = (P("dev"), P(), P(), P("dev", None))
    return jax.shard_map(local, mesh=mesh, in_specs=in_specs, out_specs=out_specs, check_vma=False)
```

time: 132 us -> 92 us (0.70)
  Pallas kernels: 33.9 us -> 86 us
  waiting for transfers between devices: 40.4 us -> 0 us
  matrix products: 24.3 us -> 0 us
  other arithmetic: 16.7 us -> 3.65 us
  starting transfers between devices: 11.8 us -> 0 us
  local copies, waits for them, and re-layouts: 2.94 us -> 1.49 us
    pallas_call x1, Pallas kernels: 33.9 us -> 86 us  [local(): pl.pallas_call(functools.partial(step_kernel, line, plane, cap), out_shap...]
    all_to_all x2 -> x0, waiting for transfers between devices: 40.4 us -> none  [the longest x1 20.9 us: local(): lax.all_to_all(payload, 'dev', split_axis=0, concat_axis=0, tiled=True)]
    dot_general x13 -> x0, matrix products: 24.3 us -> none  [the longest x1 3.97 us: local(): lax.dot_general(select, returned, (((0,), (0,)), ((), ())), preferred_ele...]
    all_to_all x2 -> x0, starting transfers between devices: 11.8 us -> none  [the longest x1 7.09 us: local(): lax.all_to_all(payload, 'dev', split_axis=0, concat_axis=0, tiled=True)]
    reduce_sum x5 -> x0, other arithmetic: 8.69 us -> none  [the longest x1 5.26 us: owner(): jnp.sum(jnp.where(table_ids[:, None, :] == which, recip[:, None, :], 0.0)...]
    reshape x4 -> x0, local copies, waits for them, and re-layouts: 1.5 us -> none  [the longest x1 1.29 us: local(): dquery.reshape(local_clusters, devices, capacity, width)]
    convert_element_type x5 -> x2, other arithmetic: 4.48 us -> 3.65 us  [the longest x1 2.93 us: local(): big.astype(F32)]
  transfers between devices with their start and end apart: 2 -> 0, of which waited for: 2 -> 0; matrix products, arithmetic and copies ran while one was open for 9% -> 0% of each run, Pallas kernels for 0% -> 0%
where the time goes in v1:
time: 92 us; the launch traced here: 91.8 us
  Pallas kernels  86 us (93%)
  other arithmetic  3.65 us (4%)
  local copies, waits for them, and re-layouts  1.49 us (2%)
    pallas_call x1, Pallas kernels, local(): pl.pallas_call(functools.partial(step_kernel, line, plane, cap), out_shap...  86 us
    convert_element_type x1, other arithmetic, local(): big.astype(F32)  2.93 us

profile of v1, /device:TPU:1, one launch (start us, length us, event | category | flops | bytes accessed | tf_op | source)
XLA Modules:
  0.0 91.8 jit_solution(10223823805494388879)
XLA Ops:
  0.6 86.0 %step.1 = (f32[1,16]{1,0:T(1,128)}, bf16[1024,512]{1,0:T(8,128)(2,1)}, bf16[512,128]{1,0:T(8,128)(2,1)}, f32[16,128,128]{2,1,0:T(8,128)}) custom-call(bf16[512,1024]{1,0:T(8,128)(2,1)} %features_hbm.1, bf16[1024,512]{1,0:T(8,128)(2,1)} %w_hidden_hbm.1, bf16[512,128]{1,0:T(8,128)(2,1)} %w_out_hbm.1, bf16[16,128,128]{2,1,0:T(8,128)(2,1)} %bitcast.7, ...), custom_call_target="tpu_custom_call" | custom-call | tf_op jit(solution)/shard_map/step/pallas_call | solution.py:609
  86.7 0.0 copy-start.1
  86.7 0.0 copy-start.2
  86.7 0.0 copy-start
  86.7 2.9 %convert_element_type.6 = f32[1024,512]{1,0:T(8,128)} convert(bf16[1024,512]{1,0:T(8,128)(2,1)} %get-tuple-element.9) | non-fusion elementwise | flops 524288 | bytes 3145728 | tf_op jit(solution)/shard_map/convert_element_type | solution.py:693
  89.6 0.0 copy-done.1
  89.6 0.7 convert_element_type.7
  90.4 0.0 copy-done.2
  90.4 0.5 copy.15
  90.9 0.0 copy-done
  90.9 1.0 %copy.16 = f32[2048,128]{1,0:T(8,128)} copy(f32[2048,128]{1,0:T(8,128)S(1)} %bitcast.6) | data formatting | bytes 2097152
Async XLA Ops:
  86.7 3.0 %copy-start.1 = (bf16[512,128]{1,0:T(8,128)(2,1)S(1)}, bf16[512,128]{1,0:T(8,128)(2,1)}, u32[]{:S(2)}) copy-start(bf16[512,128]{1,0:T(8,128)(2,1)} %get-tuple-element.10) | copy-start | bytes 393220
  86.7 3.7 %copy-start.2 = (f32[1,16]{1,0:T(1,128)S(1)}, f32[1,16]{1,0:T(1,128)}, u32[]{:S(2)}) copy-start(f32[1,16]{1,0:T(1,128)} %get-tuple-element.8) | copy-start | bytes 196
  86.7 4.2 %copy-start = (f32[16,128,128]{2,1,0:T(8,128)S(1)}, f32[16,128,128]{2,1,0:T(8,128)}, u32[]{:S(2)}) copy-start(f32[16,128,128]{2,1,0:T(8,128)} %get-tuple-element.11) | copy-start | bytes 3145732
